TPU v7x, 256 devices: a whole 4x4x8 slice. The times are simulated.
256 devices in a mesh: fsdp: 16 (over y, x), ctx: 16 (over z, core).
Axes of the slice: x: 4, y: 4, z: 8, core: 2. Of those that a mesh axis runs over, the one named last changes fastest.
Arguments:
- queries: bfloat16 [32768, 2048], P(('fsdp', 'ctx')), may hold values from -80 to 80
- keys: bfloat16 [32768, 2048], P(('fsdp', 'ctx')), may hold values from -4 to 4
- values: bfloat16 [32768, 2048], P(('fsdp', 'ctx')), may hold values from -6 to 6
- out_weight: bfloat16 [2048, 4096], P('fsdp'), may hold values from -0.125 to 0.125
- sessions: int32 [16, 2048], P('fsdp'), may hold values from 0 to 2, never falling along the last dimension, each value on 1 to 1536 neighbouring positions
Outputs:
- output: bfloat16 [32768, 4096], P(('fsdp', 'ctx'))
Inputs may be any that keep to these rules, and one draw needn't show every extreme that they name: Along each slab the session number never falls; each of the 3 sessions holds 1 to 1536 tokens and one holds exactly 1536.
All inputs are finite; a program needn't handle non-finite values.
Results may differ from a plain program's by a relative error of at most 0.007.
Values may be sent and summed in bfloat16 or wider, within the bound.
No kernel may reach another device: no remote copies, remote signals or barrier semaphores. Data moves between devices by JAX's collectives and lax.ppermute only.
A program may use at most 128 MiB of HBM per device.

v0:
```python
import math
import jax
import jax.numpy as jnp
from jax import lax
from jax.sharding import PartitionSpec as P

HDIM = 128


def per_device(queries, keys, values, out_weight, sessions):
    tokens_here = queries.shape[0]
    width = queries.shape[1]
    heads_here = width // HDIM
    scale = 1.0 / math.sqrt(HDIM)
    slab_ids = sessions[0]
    first_token = lax.axis_index("ctx") * tokens_here
    my_positions = first_token + jnp.arange(tokens_here, dtype=jnp.int32)
    my_ids = lax.dynamic_slice_in_dim(slab_ids, first_token, tokens_here)
    query_heads = jnp.transpose(queries.reshape(tokens_here, heads_here, HDIM), (1, 0, 2))
    start_state = (
        jnp.full((heads_here, tokens_here), -1e30, jnp.float32),
        jnp.zeros((heads_here, tokens_here), jnp.float32),
        jnp.zeros((heads_here, tokens_here, HDIM), jnp.float32),
    )
    key_piece = lax.all_gather(keys, "ctx", axis=0, tiled=True)
    value_piece = lax.all_gather(values, "ctx", axis=0, tiled=True)
    count = key_piece.shape[0]
    key_positions = jnp.arange(count, dtype=jnp.int32)
    allowed = (my_ids[:, None] == slab_ids[None, :]) & (
        key_positions[None, :] <= my_positions[:, None]
    )

    def update(current):
        key_heads = jnp.transpose(key_piece.reshape(count, heads_here, HDIM), (1, 0, 2))
        value_heads = jnp.transpose(value_piece.reshape(count, heads_here, HDIM), (1, 0, 2))

        def one_head(operands):
            query_head, key_head, value_head, row_max, row_total, accum = operands
            scores = jnp.dot(query_head, key_head.T, preferred_element_type=jnp.float32) * scale
            scores = jnp.where(allowed, scores, jnp.float32(-1e30))
            new_max = jnp.maximum(row_max, jnp.max(scores, axis=1))
            weights = jnp.where(allowed, jnp.exp(scores - new_max[:, None]), jnp.float32(0.0))
            factor = jnp.exp(row_max - new_max)
            new_total = row_total * factor + jnp.sum(weights, axis=1)
            added = jnp.dot(
                weights.astype(jnp.bfloat16), value_head, preferred_element_type=jnp.float32
            )
            return (new_max, new_total, accum * factor[:, None] + added)

        return lax.map(one_head, (query_heads, key_heads, value_heads) + tuple(current))

    row_max, row_total, accum = lax.cond(
        jnp.any(allowed), update, lambda current: current, start_state
    )
    finished = accum / row_total[:, :, None]
    attended = jnp.transpose(finished, (1, 0, 2)).reshape(tokens_here, width).astype(jnp.bfloat16)
    piece = lax.all_gather(out_weight, "fsdp", axis=0, tiled=True)
    projected = jnp.dot(attended, piece, preferred_element_type=jnp.float32)
    return projected.astype(jnp.bfloat16)


def solution(mesh):
    return jax.shard_map(
        per_device,
        mesh=mesh,
        in_specs=(
            P(("fsdp", "ctx"), None),
            P(("fsdp", "ctx"), None),
            P(("fsdp", "ctx"), None),
            P("fsdp", None),
            P("fsdp", None),
        ),
        out_specs=P(("fsdp", "ctx"), None),
        check_vma=False,
    )
```

profile of v0, /device:TPU:1, one launch (start us, length us, event | category | flops | bytes accessed | tf_op | source)
XLA Modules:
  0.0 274.5 jit_solution(3808026801106439446)
XLA Ops:
  6.5 2.0 copy.8
  8.7 2.0 copy.9
  10.8 0.7 all-gather.8.cloned.1.call-update
  11.5 0.7 dynamic-slice_bitcast_fusion
  12.1 1.7 fusion.16
  14.4 1.3 copy.10
  15.7 63.8 %all-gather.4.cloned.1.call-done = bf16[2048,2048]{0,1:T(8,128)(2,1)} async-done(((bf16[128,2048]{0,1:T(8,128)(2,1)}), bf16[2048,2048]{0,1:T(8,128)(2,1)}) %all-gather.4.cloned.1.call-update) | async-done | bytes 8388624 | tf_op jit(solution)/shard_map/all_gather | solution.py:25
  79.5 64.4 %all-gather.6.cloned.1.call-done = bf16[2048,2048]{0,1:T(8,128)(2,1)} async-done(((bf16[128,2048]{0,1:T(8,128)(2,1)}), bf16[2048,2048]{0,1:T(8,128)(2,1)}) %all-gather.6.cloned.1.call-update) | async-done | bytes 8388624 | tf_op jit(solution)/shard_map/all_gather | solution.py:26
  143.9 86.1 %conditional.1 = (f32[16,128]{1,0:T(8,128)}, f32[16,128,128]{1,2,0:T(8,128)}) conditional(s32[]{:T(128)} %convert_element_type.18, () %tuple.17, (bf16[2048,2048]{0,1:T(8,128)(2,1)}, bf16[2048,2048]{0,1:T(8,128)(2,1)}, bf16[16,128,128]{1,2,0:T(8,128)(2,1)S(1)}, pred[128,2048]{1,0:T(32,128)(4,1)S(1)}) %tuple.49), branch_computations={%region_1.0_spmd, %region_2.7_spmd} | conditional | flops 136593792 | bytes 5349073 | solution.py:52
  143.9 86.1 %while.11 = (s32[]{:T(128)}, f32[16,128]{1,0:T(8,128)}, f32[16,128,128]{1,2,0:T(8,128)}, bf16[16,128,128]{1,2,0:T(8,128)(2,1)S(1)}, bf16[16,2048,128]{1,2,0:T(8,...) while((s32[]{:T(128)}, f32[16,128]{1,0:T(8,128)}, ...), condition=%wide.region_6.6_spmd, body=%wide.region_3.5_spmd.sunk | while | flops 136593792 | bytes 5348977 | solution.py:50
  143.9 1.5 fusion.28
  145.8 1.3 dynamic_update_slice.12
  147.1 1.4 fusion.30
  148.7 0.6 constant_dynamic-update-slice_fusion.2
  149.3 1.5 fusion.28
  151.2 1.3 dynamic_update_slice.12
  152.5 1.4 fusion.30
  154.0 0.6 constant_dynamic-update-slice_fusion.2
  154.7 1.5 fusion.28
  156.6 1.3 dynamic_update_slice.12
  157.9 1.4 fusion.30
  159.5 0.6 constant_dynamic-update-slice_fusion.2
  160.1 1.5 fusion.28
  162.0 1.3 dynamic_update_slice.12
  163.3 1.5 fusion.30
  165.5 1.5 fusion.28
  167.4 1.3 dynamic_update_slice.12
  168.7 1.5 fusion.30
  170.9 1.5 fusion.28
  172.8 1.3 dynamic_update_slice.12
  174.1 1.5 fusion.30
  176.2 1.5 fusion.28
  178.1 1.3 dynamic_update_slice.12
  179.4 1.4 fusion.30
  181.6 1.5 fusion.28
  183.5 1.3 dynamic_update_slice.12
  184.8 1.4 fusion.30
  187.0 1.5 fusion.28
  188.9 1.3 dynamic_update_slice.12
  190.2 1.5 fusion.30
  192.4 1.5 fusion.28
  194.2 1.3 dynamic_update_slice.12
  195.5 1.4 fusion.30
  197.7 1.5 fusion.28
  199.6 1.3 dynamic_update_slice.12
  200.9 1.4 fusion.30
  203.1 1.5 fusion.28
  205.0 1.3 dynamic_update_slice.12
  206.3 1.4 fusion.30
  208.5 1.5 fusion.28
  210.4 1.3 dynamic_update_slice.12
  211.7 1.4 fusion.30
  213.9 1.5 fusion.28
  215.8 1.3 dynamic_update_slice.12
  217.1 1.4 fusion.30
  219.3 1.5 fusion.28
  221.2 1.3 dynamic_update_slice.12
  222.5 1.4 fusion.30
  224.7 1.5 fusion.28
  226.6 1.3 dynamic_update_slice.12
  227.9 1.4 fusion.30
  230.0 1.3 divide_convert_fusion
  231.4 27.4 %all-gather.8.cloned.1.call-done = bf16[2048,4096]{1,0:T(8,128)(2,1)} async-done(((bf16[128,4096]{1,0:T(8,128)(2,1)}), bf16[2048,4096]{1,0:T(8,128)(2,1)}) %all-gather.8.cloned.1.call-update) | async-done | bytes 16777232 | tf_op jit(solution)/shard_map/all_gather | solution.py:57
  258.8 9.1 %convolution_convert_fusion = bf16[128,4096]{1,0:T(8,128)(2,1)} fusion(bf16[128,2048]{0,1:T(8,128)(2,1)S(1)} %bitcast.45, bf16[2048,4096]{1,0:T(8,128)(2,1)} %all-gather.8.cloned.1.call-done), kind=kOutput, calls=%fused_computation.22 | convolution fusion | flops 2148007936 | bytes 18350080 | tf_op jit(solution)/shard_map/dot_general | solution.py:58
  (85 shorter events, 16.3 us)
Async XLA Ops:
  6.5 73.0 %all-gather.4.cloned.1.call-start = ((), (), s32[]{:S(2)}) async-start(), calls=%async_computation | async-start | bytes 8912896 | tf_op jit(solution)/shard_map/all_gather | solution.py:25
  8.6 135.3 %all-gather.6.cloned.1.call-start = ((), (), s32[]{:S(2)}) async-start(), calls=%async_computation.1 | async-start | bytes 8912896 | tf_op jit(solution)/shard_map/all_gather | solution.py:26
  10.7 248.1 %all-gather.8.cloned.1.call-start = ((), (), s32[]{:S(2)}) async-start(), calls=%async_computation.2 | async-start | bytes 17825792 | tf_op jit(solution)/shard_map/all_gather | solution.py:57
Sparse Core Ops, SparseCore 0:
  9.1 70.3 all-gather.3
  81.2 62.6 all-gather.5
  146.4 112.4 all-gather.7
where the time goes:
time: 277 us; the launch traced here: 274 us
  waiting for transfers between devices  156 us (56%)
  matrix products  56 us (20%)
  local copies, waits for them, and re-layouts  38.5 us (14%)
  between operations  13.7 us (5%)
  other arithmetic  9.54 us (3%)
    all_gather x1, waiting for transfers between devices, per_device(): value_piece = lax.all_gather(values, 'ctx', axis=0, tiled=True)  64.4 us
    all_gather x1, waiting for transfers between devices, per_device(): key_piece = lax.all_gather(keys, 'ctx', axis=0, tiled=True)  63.8 us
    dynamic_update_slice x48, local copies, waits for them, and re-layouts, update(): lax.map(one_head, (query_heads, key_heads, value_heads) + tuple(current))  32.4 us
    all_gather x1, waiting for transfers between devices, per_device(): piece = lax.all_gather(out_weight, 'fsdp', axis=0, tiled=True)  27.4 us
    dot_general x16, matrix products, one_head(): jnp.dot(query_head, key_head.T, preferred_element_type=jnp.float32) * scale  23.7 us
    dot_general x16, matrix products, one_head(): jnp.dot(weights.astype(jnp.bfloat16), value_head, preferred_element_type=...  23.2 us
    dot_general x1, matrix products, per_device(): projected = jnp.dot(attended, piece, preferred_element_type=jnp.float32)  9.1 us
    reduce_sum x16, other arithmetic, one_head(): new_total = row_total * factor + jnp.sum(weights, axis=1)  6.21 us
  transfers between devices with their start and end apart: 3, of which 3 were waited for; matrix products, arithmetic and copies ran while one was open for 34% of the time, Pallas kernels for 0%

commit v1 on v0

--- a/solution.py
+++ b/solution.py
@@ -3,6 +3,7 @@
 import jax.numpy as jnp
 from jax import lax
 from jax.sharding import PartitionSpec as P
+from jax.lax import axis_index, axis_size, ppermute
 
 HDIM = 128
 
@@ -54,7 +55,34 @@
     )
     finished = accum / row_total[:, :, None]
     attended = jnp.transpose(finished, (1, 0, 2)).reshape(tokens_here, width).astype(jnp.bfloat16)
-    piece = lax.all_gather(out_weight, "fsdp", axis=0, tiled=True)
+
+    def _play_arrays(incoming_x, chip_axis):
+        side_arr = axis_size(chip_axis)
+        u_next = axis_index(chip_axis)
+        mid_arr, x_next, newest = (side_arr, u_next, incoming_x.shape[0])
+        items = tuple(((num, (num + 1) % mid_arr) for num in range(mid_arr)))
+        inbox = tuple(((num, (num - 1) % mid_arr) for num in range(mid_arr)))
+        v1 = jnp.zeros(
+            (*incoming_x.shape[:0], mid_arr * newest, *incoming_x.shape[1:]), incoming_x.dtype
+        )
+        v1 = lax.dynamic_update_slice_in_dim(v1, incoming_x, x_next * newest, axis=0)
+        arr_now = carry = incoming_x
+        known = mid_arr // 2
+        to_i = 1
+        while to_i < known + 1:
+            arr_now = ppermute(arr_now, chip_axis, perm=items)
+            v1 = lax.dynamic_update_slice_in_dim(
+                v1, arr_now, (x_next - to_i) % mid_arr * newest, axis=0
+            )
+            if to_i < mid_arr - known:
+                carry = ppermute(carry, axis_name=chip_axis, perm=inbox)
+                v1 = lax.dynamic_update_slice_in_dim(
+                    v1, carry, (x_next + to_i) % mid_arr * newest, axis=0
+                )
+            to_i += 1
+        return v1
+
+    piece = _play_arrays(out_weight, "fsdp")
     projected = jnp.dot(attended, piece, preferred_element_type=jnp.float32)
     return projected.astype(jnp.bfloat16)
 

time: 277 us -> 320 us (1.16)
  the two profiles are of different devices: /device:TPU:1 before, /device:TPU:128 now
where the time goes in v1:
time: 320 us; the launch traced here: 318 us
  waiting for transfers between devices  132 us (41%)
  local copies, waits for them, and re-layouts  67.5 us (21%)
  matrix products  56.1 us (18%)
  starting transfers between devices  38.8 us (12%)
  between operations  14.1 us (4%)
  other arithmetic  8.87 us (3%)
    ppermute x8, waiting for transfers between devices, _play_arrays(): arr_now = ppermute(arr_now, chip_axis, perm=items)  123 us
    ppermute x7, starting transfers between devices, _play_arrays(): carry = ppermute(carry, axis_name=chip_axis, perm=inbox)  37.2 us
    dynamic_update_slice x48, local copies, waits for them, and re-layouts, update(): lax.map(one_head, (query_heads, key_heads, value_heads) + tuple(current))  32.4 us
    dot_general x16, matrix products, one_head(): jnp.dot(query_head, key_head.T, preferred_element_type=jnp.float32) * scale  23.9 us
    dot_general x16, matrix products, one_head(): jnp.dot(weights.astype(jnp.bfloat16), value_head, preferred_element_type=...  23.1 us
    dynamic_update_slice x7, local copies, waits for them, and re-layouts, _play_arrays(): lax.dynamic_update_slice_in_dim(v1, carry, (x_next + to_i) % mid_arr * ne...  11.2 us
    dynamic_update_slice x8, local copies, waits for them, and re-layouts, _play_arrays(): lax.dynamic_update_slice_in_dim(v1, arr_now, (x_next - to_i) % mid_arr *...  9.92 us
    ppermute x7, waiting for transfers between devices, _play_arrays(): carry = ppermute(carry, axis_name=chip_axis, perm=inbox)  9.38 us
  transfers between devices with their start and end apart: 17, of which 12 were waited for; matrix products, arithmetic and copies ran while one was open for 11% of the time, Pallas kernels for 0%

profile of v1, /device:TPU:128, one launch (start us, length us, event | category | flops | bytes accessed | tf_op | source)
XLA Modules:
  0.0 317.9 jit_solution(12073623276625316916)
XLA Ops:
  6.5 2.1 copy.8
  8.8 2.0 copy.9
  10.8 1.6 collective-permute-start
  12.4 3.9 %collective-permute-start.1 = (bf16[128,4096]{1,0:T(8,128)(2,1)}, bf16[128,4096]{1,0:T(8,128)(2,1)}, u32[]{:S(2)}, u32[]{:S(2)}) collective-permute-start(bf16[128,4096]{1,0:T(8,128)(2,1)} %param.12), channel_id=1, source_target_pairs={{0,240},{16,0},{32,16},{48,32},{64,48},{80,64},{96,80},{112,96},{1... | collective-permute-start | bytes 3145736 | tf_op jit(solution)/shard_map/ppermute | solution.py:78
  16.2 23.2 %collective-permute-done = bf16[128,4096]{1,0:T(8,128)(2,1)S(1)} collective-permute-done((bf16[128,4096]{1,0:T(8,128)(2,1)}, bf16[128,4096]{1,0:T(8,128)(2,1)S(1)}, u32[]{:S(2)}, u32[]{:S(2)}) %collective-permute-start) | collective-permute-done | bytes 1048608 | tf_op jit(solution)/shard_map/ppermute | solution.py:73
  39.5 5.3 %collective-permute-start.3 = (bf16[128,4096]{1,0:T(8,128)(2,1)}, bf16[128,4096]{1,0:T(8,128)(2,1)}, u32[]{:S(2)}, u32[]{:S(2)}) collective-permute-start(bf16[128,4096]{1,0:T(8,128)(2,1)} %collective-permute-done.1), channel_id=1, source_target_pairs={{0,240},{16,0},{32,16},{48,32},{64,48},{80,64},{96,80},{112,96},{1... | collective-permute-start | bytes 3145736 | tf_op jit(solution)/shard_map/ppermute | solution.py:78
  44.8 22.2 %collective-permute-done.2 = bf16[128,4096]{1,0:T(8,128)(2,1)S(1)} collective-permute-done((bf16[128,4096]{1,0:T(8,128)(2,1)S(1)}, bf16[128,4096]{1,0:T(8,128)(2,1)S(1)}, u32[]{:S(2)}, u32[]{:S(2)}) %collective-permute-start.2) | collective-permute-done | bytes 1048608 | tf_op jit(solution)/shard_map/ppermute | solution.py:73
  67.7 5.3 %collective-permute-start.5 = (bf16[128,4096]{1,0:T(8,128)(2,1)}, bf16[128,4096]{1,0:T(8,128)(2,1)}, u32[]{:S(2)}, u32[]{:S(2)}) collective-permute-start(bf16[128,4096]{1,0:T(8,128)(2,1)} %collective-permute-done.3), channel_id=1, source_target_pairs={{0,240},{16,0},{32,16},{48,32},{64,48},{80,64},{96,80},{112,96},{1... | collective-permute-start | bytes 3145736 | tf_op jit(solution)/shard_map/ppermute | solution.py:78
  73.0 6.0 %broadcast_in_dim.23 = bf16[2048,4096]{1,0:T(8,128)(2,1)} broadcast(bf16[]{:T(256)} %constant.136.clone.1), dimensions={} | broadcast | bytes 16777218 | tf_op jit(solution)/shard_map/broadcast_in_dim | solution.py:65
  80.1 13.5 %collective-permute-done.4 = bf16[128,4096]{1,0:T(8,128)(2,1)S(1)} collective-permute-done((bf16[128,4096]{1,0:T(8,128)(2,1)S(1)}, bf16[128,4096]{1,0:T(8,128)(2,1)S(1)}, u32[]{:S(2)}, u32[]{:S(2)}) %collective-permute-start.4) | collective-permute-done | bytes 1048608 | tf_op jit(solution)/shard_map/ppermute | solution.py:73
  95.3 2.1 copy.10
  97.4 2.3 constant_dynamic-update-slice_fusion.15
  99.6 5.4 %collective-permute-start.7 = (bf16[128,4096]{1,0:T(8,128)(2,1)}, bf16[128,4096]{1,0:T(8,128)(2,1)S(1)}, u32[]{:S(2)}, u32[]{:S(2)}) collective-permute-start(bf16[128,4096]{1,0:T(8,128)(2,1)} %collective-permute-done.5), channel_id=1, source_target_pairs={{0,240},{16,0},{32,16},{48,32},{64,48},{80,64},{96,80},{112,96},{1... | collective-permute-start | bytes 3145736 | tf_op jit(solution)/shard_map/ppermute | solution.py:78
  105.0 2.3 constant_dynamic-update-slice_fusion.14
  107.3 12.0 %collective-permute-done.6 = bf16[128,4096]{1,0:T(8,128)(2,1)S(1)} collective-permute-done((bf16[128,4096]{1,0:T(8,128)(2,1)S(1)}, bf16[128,4096]{1,0:T(8,128)(2,1)S(1)}, u32[]{:S(2)}, u32[]{:S(2)}) %collective-permute-start.6) | collective-permute-done | bytes 1048608 | tf_op jit(solution)/shard_map/ppermute | solution.py:73
  120.4 2.3 constant_dynamic-update-slice_fusion.12
  122.6 2.3 collective-permute-done.7
  124.9 5.7 %collective-permute-start.9 = (bf16[128,4096]{1,0:T(8,128)(2,1)S(1)}, bf16[128,4096]{1,0:T(8,128)(2,1)S(1)}, u32[]{:S(2)}, u32[]{:S(2)}) collective-permute-start(bf16[128,4096]{1,0:T(8,128)(2,1)S(1)} %collective-permute-done.7), channel_id=1, source_target_pairs={{0,240},{16,0},{32,16},{48,32},{64,48},{80,64},{96,80},{112,96},{1... | collective-permute-start | bytes 3145736 | tf_op jit(solution)/shard_map/ppermute | solution.py:78
  131.7 12.3 %collective-permute-done.8 = bf16[128,4096]{1,0:T(8,128)(2,1)S(1)} collective-permute-done((bf16[128,4096]{1,0:T(8,128)(2,1)S(1)}, bf16[128,4096]{1,0:T(8,128)(2,1)S(1)}, u32[]{:S(2)}, u32[]{:S(2)}) %collective-permute-start.8) | collective-permute-done | bytes 1048608 | tf_op jit(solution)/shard_map/ppermute | solution.py:73
  144.0 2.3 constant_dynamic-update-slice_fusion.10
  147.4 1.9 collective-permute-done.9
  149.3 5.8 %collective-permute-start.11 = (bf16[128,4096]{1,0:T(8,128)(2,1)S(1)}, bf16[128,4096]{1,0:T(8,128)(2,1)S(1)}, u32[]{:S(2)}, u32[]{:S(2)}) collective-permute-start(bf16[128,4096]{1,0:T(8,128)(2,1)S(1)} %collective-permute-done.9), channel_id=1, source_target_pairs={{0,240},{16,0},{32,16},{48,32},{64,48},{80,64},{96,80},{112,96},{1... | collective-permute-start | bytes 3145736 | tf_op jit(solution)/shard_map/ppermute | solution.py:78
  156.2 11.7 %collective-permute-done.10 = bf16[128,4096]{1,0:T(8,128)(2,1)S(1)} collective-permute-done((bf16[128,4096]{1,0:T(8,128)(2,1)S(1)}, bf16[128,4096]{1,0:T(8,128)(2,1)S(1)}, u32[]{:S(2)}, u32[]{:S(2)}) %collective-permute-start.10) | collective-permute-done | bytes 1048608 | tf_op jit(solution)/shard_map/ppermute | solution.py:73
  170.0 2.9 collective-permute-done.11
  172.9 5.8 %collective-permute-start.13 = (bf16[128,4096]{1,0:T(8,128)(2,1)S(1)}, bf16[128,4096]{1,0:T(8,128)(2,1)S(1)}, u32[]{:S(2)}, u32[]{:S(2)}) collective-permute-start(bf16[128,4096]{1,0:T(8,128)(2,1)S(1)} %collective-permute-done.11), channel_id=1, source_target_pairs={{0,240},{16,0},{32,16},{48,32},{64,48},{80,64},{96,80},{112,96},{1... | collective-permute-start | bytes 3145736 | tf_op jit(solution)/shard_map/ppermute | solution.py:78
  179.8 11.4 %collective-permute-done.12 = bf16[128,4096]{1,0:T(8,128)(2,1)S(1)} collective-permute-done((bf16[128,4096]{1,0:T(8,128)(2,1)S(1)}, bf16[128,4096]{1,0:T(8,128)(2,1)S(1)}, u32[]{:S(2)}, u32[]{:S(2)}) %collective-permute-start.12) | collective-permute-done | bytes 1048608 | tf_op jit(solution)/shard_map/ppermute | solution.py:73
  193.3 2.3 collective-permute-done.13
  196.7 16.5 %collective-permute-done.14 = bf16[128,4096]{1,0:T(8,128)(2,1)S(1)} collective-permute-done((bf16[128,4096]{1,0:T(8,128)(2,1)S(1)}, bf16[128,4096]{1,0:T(8,128)(2,1)S(1)}, u32[]{:S(2)}, u32[]{:S(2)}) %collective-permute-start.14) | collective-permute-done | bytes 1048608 | tf_op jit(solution)/shard_map/ppermute | solution.py:73
  214.4 86.2 %conditional.1 = (f32[16,128]{1,0:T(8,128)}, f32[16,128,128]{1,2,0:T(8,128)}) conditional(s32[]{:T(128)} %convert_element_type.18, () %tuple.17, (bf16[2048,2048]{0,1:T(8,128)(2,1)}, bf16[2048,2048]{0,1:T(8,128)(2,1)}, bf16[16,128,128]{1,2,0:T(8,128)(2,1)}, pred[128,2048]{1,0:T(32,128)(4,1)S(1)}) %tuple.47), branch_computations={%region_1.0_spmd, %region_2.7_spmd} | conditional | flops 136593792 | bytes 5349073 | solution.py:53
  214.4 86.2 %while.11 = (s32[]{:T(128)}, f32[16,128]{1,0:T(8,128)}, f32[16,128,128]{1,2,0:T(8,128)}, bf16[16,128,128]{1,2,0:T(8,128)(2,1)}, bf16[16,2048,128]{1,2,0:T(8,128)...) while((s32[]{:T(128)}, f32[16,128]{1,0:T(8,128)}, ...), condition=%wide.region_6.6_spmd, body=%wide.region_3.5_spmd.sunk | while | flops 136593792 | bytes 5348977 | solution.py:51
  214.4 1.5 fusion.29
  217.6 1.4 fusion.31
  219.8 1.5 fusion.29
  223.0 1.4 fusion.31
  225.2 1.5 fusion.29
  228.4 1.4 fusion.31
  230.6 1.5 fusion.29
  233.8 1.4 fusion.31
  236.0 1.5 fusion.29
  239.2 1.4 fusion.31
  241.4 1.5 fusion.29
  244.6 1.4 fusion.31
  246.8 1.5 fusion.29
  250.0 1.4 fusion.31
  252.2 1.5 fusion.29
  255.4 1.4 fusion.31
  257.6 1.5 fusion.29
  260.8 1.4 fusion.31
  263.0 1.5 fusion.29
  266.2 1.4 fusion.31
  268.3 1.5 fusion.29
  271.5 1.4 fusion.31
  273.7 1.5 fusion.29
  276.9 1.4 fusion.31
  279.1 1.5 fusion.29
  282.3 1.4 fusion.31
  284.5 1.5 fusion.29
  287.7 1.4 fusion.31
  289.9 1.5 fusion.29
  293.1 1.4 fusion.31
  295.3 1.5 fusion.29
  298.4 1.4 fusion.31
  300.6 1.3 divide_convert_fusion
  302.0 9.1 %convolution_convert_fusion = bf16[128,4096]{1,0:T(8,128)(2,1)} fusion(bf16[128,2048]{0,1:T(8,128)(2,1)S(1)} %bitcast.45, bf16[2048,4096]{1,0:T(8,128)(2,1)} %constant_dynamic-update-slice_fusion.1), kind=kOutput, calls=%fused_computation.22 | convolution fusion | flops 2148007936 | bytes 18350080 | tf_op jit(solution)/shard_map/dot_general | solution.py:86
  (135 shorter events, 53.8 us)
Async XLA Ops:
  6.5 72.4 %copy-start = (bf16[128,4096]{1,0:T(8,128)(2,1)S(1)}, bf16[128,4096]{1,0:T(8,128)(2,1)}, u32[]{:S(2)}) copy-start(bf16[128,4096]{1,0:T(8,128)(2,1)} %param.12) | copy-start | bytes 3145732
  6.5 87.1 %copy-start.2 = (s32[1,2048]{1,0:T(1,128)S(1)}, s32[1,2048]{1,0:T(1,128)}, u32[]{:S(2)}) copy-start(s32[1,2048]{1,0:T(1,128)} %param.13) | copy-start | bytes 24580
  6.5 207.9 %all-gather.3.cloned.1.call-start = ((), (), s32[]{:S(2)}) async-start(), calls=%async_computation | async-start | bytes 8912896 | tf_op jit(solution)/shard_map/all_gather | solution.py:26
  8.7 205.7 %all-gather.5.cloned.1.call-start = ((), (), s32[]{:S(2)}) async-start(), calls=%async_computation.1 | async-start | bytes 8912896 | tf_op jit(solution)/shard_map/all_gather | solution.py:27
  10.8 28.7 %collective-permute-start = (bf16[128,4096]{1,0:T(8,128)(2,1)}, bf16[128,4096]{1,0:T(8,128)(2,1)S(1)}, u32[]{:S(2)}, u32[]{:S(2)}) collective-permute-start(bf16[128,4096]{1,0:T(8,128)(2,1)} %param.12), channel_id=1, source_target_pairs={{0,16},{16,32},{32,48},{48,64},{64,80},{80,96},{96,112},{112,128},... | collective-permute-start | bytes 3145736 | tf_op jit(solution)/shard_map/ppermute | solution.py:73
  12.4 27.1 %collective-permute-start.1 = (bf16[128,4096]{1,0:T(8,128)(2,1)}, bf16[128,4096]{1,0:T(8,128)(2,1)}, u32[]{:S(2)}, u32[]{:S(2)}) collective-permute-start(bf16[128,4096]{1,0:T(8,128)(2,1)} %param.12), channel_id=1, source_target_pairs={{0,240},{16,0},{32,16},{48,32},{64,48},{80,64},{96,80},{112,96},{1... | collective-permute-start | bytes 3145736 | tf_op jit(solution)/shard_map/ppermute | solution.py:78
  39.5 5.4 %copy-start.1 = (bf16[128,4096]{1,0:T(8,128)(2,1)}, bf16[128,4096]{1,0:T(8,128)(2,1)S(1)}, u32[]{:S(2)}) copy-start(bf16[128,4096]{1,0:T(8,128)(2,1)S(1)} %collective-permute-done) | copy-start | bytes 3145732
  39.5 27.5 %collective-permute-start.2 = (bf16[128,4096]{1,0:T(8,128)(2,1)S(1)}, bf16[128,4096]{1,0:T(8,128)(2,1)S(1)}, u32[]{:S(2)}, u32[]{:S(2)}) collective-permute-start(bf16[128,4096]{1,0:T(8,128)(2,1)S(1)} %collective-permute-done), channel_id=1, source_target_pairs={{0,16},{16,32},{32,48},{48,64},{64,80},{80,96},{96,112},{112,128},... | collective-permute-start | bytes 3145736 | tf_op jit(solution)/shard_map/ppermute | solution.py:73
  39.5 28.2 %collective-permute-start.3 = (bf16[128,4096]{1,0:T(8,128)(2,1)}, bf16[128,4096]{1,0:T(8,128)(2,1)}, u32[]{:S(2)}, u32[]{:S(2)}) collective-permute-start(bf16[128,4096]{1,0:T(8,128)(2,1)} %collective-permute-done.1), channel_id=1, source_target_pairs={{0,240},{16,0},{32,16},{48,32},{64,48},{80,64},{96,80},{112,96},{1... | collective-permute-start | bytes 3145736 | tf_op jit(solution)/shard_map/ppermute | solution.py:78
  67.0 26.6 %collective-permute-start.4 = (bf16[128,4096]{1,0:T(8,128)(2,1)S(1)}, bf16[128,4096]{1,0:T(8,128)(2,1)S(1)}, u32[]{:S(2)}, u32[]{:S(2)}) collective-permute-start(bf16[128,4096]{1,0:T(8,128)(2,1)S(1)} %collective-permute-done.2), channel_id=1, source_target_pairs={{0,16},{16,32},{32,48},{48,64},{64,80},{80,96},{96,112},{112,128},... | collective-permute-start | bytes 3145736 | tf_op jit(solution)/shard_map/ppermute | solution.py:73
  67.7 32.0 %collective-permute-start.5 = (bf16[128,4096]{1,0:T(8,128)(2,1)}, bf16[128,4096]{1,0:T(8,128)(2,1)}, u32[]{:S(2)}, u32[]{:S(2)}) collective-permute-start(bf16[128,4096]{1,0:T(8,128)(2,1)} %collective-permute-done.3), channel_id=1, source_target_pairs={{0,240},{16,0},{32,16},{48,32},{64,48},{80,64},{96,80},{112,96},{1... | collective-permute-start | bytes 3145736 | tf_op jit(solution)/shard_map/ppermute | solution.py:78
  93.6 25.7 %collective-permute-start.6 = (bf16[128,4096]{1,0:T(8,128)(2,1)S(1)}, bf16[128,4096]{1,0:T(8,128)(2,1)S(1)}, u32[]{:S(2)}, u32[]{:S(2)}) collective-permute-start(bf16[128,4096]{1,0:T(8,128)(2,1)S(1)} %collective-permute-done.4), channel_id=1, source_target_pairs={{0,16},{16,32},{32,48},{48,64},{64,80},{80,96},{96,112},{112,128},... | collective-permute-start | bytes 3145736 | tf_op jit(solution)/shard_map/ppermute | solution.py:73
  99.6 25.3 %collective-permute-start.7 = (bf16[128,4096]{1,0:T(8,128)(2,1)}, bf16[128,4096]{1,0:T(8,128)(2,1)S(1)}, u32[]{:S(2)}, u32[]{:S(2)}) collective-permute-start(bf16[128,4096]{1,0:T(8,128)(2,1)} %collective-permute-done.5), channel_id=1, source_target_pairs={{0,240},{16,0},{32,16},{48,32},{64,48},{80,64},{96,80},{112,96},{1... | collective-permute-start | bytes 3145736 | tf_op jit(solution)/shard_map/ppermute | solution.py:78
  119.3 24.8 %collective-permute-start.8 = (bf16[128,4096]{1,0:T(8,128)(2,1)S(1)}, bf16[128,4096]{1,0:T(8,128)(2,1)S(1)}, u32[]{:S(2)}, u32[]{:S(2)}) collective-permute-start(bf16[128,4096]{1,0:T(8,128)(2,1)S(1)} %collective-permute-done.6), channel_id=1, source_target_pairs={{0,16},{16,32},{32,48},{48,64},{64,80},{80,96},{96,112},{112,128},... | collective-permute-start | bytes 3145736 | tf_op jit(solution)/shard_map/ppermute | solution.py:73
  124.9 24.4 %collective-permute-start.9 = (bf16[128,4096]{1,0:T(8,128)(2,1)S(1)}, bf16[128,4096]{1,0:T(8,128)(2,1)S(1)}, u32[]{:S(2)}, u32[]{:S(2)}) collective-permute-start(bf16[128,4096]{1,0:T(8,128)(2,1)S(1)} %collective-permute-done.7), channel_id=1, source_target_pairs={{0,240},{16,0},{32,16},{48,32},{64,48},{80,64},{96,80},{112,96},{1... | collective-permute-start | bytes 3145736 | tf_op jit(solution)/shard_map/ppermute | solution.py:78
  144.0 23.8 %collective-permute-start.10 = (bf16[128,4096]{1,0:T(8,128)(2,1)S(1)}, bf16[128,4096]{1,0:T(8,128)(2,1)S(1)}, u32[]{:S(2)}, u32[]{:S(2)}) collective-permute-start(bf16[128,4096]{1,0:T(8,128)(2,1)S(1)} %collective-permute-done.8), channel_id=1, source_target_pairs={{0,16},{16,32},{32,48},{48,64},{64,80},{80,96},{96,112},{112,128},... | collective-permute-start | bytes 3145736 | tf_op jit(solution)/shard_map/ppermute | solution.py:73
  149.3 23.6 %collective-permute-start.11 = (bf16[128,4096]{1,0:T(8,128)(2,1)S(1)}, bf16[128,4096]{1,0:T(8,128)(2,1)S(1)}, u32[]{:S(2)}, u32[]{:S(2)}) collective-permute-start(bf16[128,4096]{1,0:T(8,128)(2,1)S(1)} %collective-permute-done.9), channel_id=1, source_target_pairs={{0,240},{16,0},{32,16},{48,32},{64,48},{80,64},{96,80},{112,96},{1... | collective-permute-start | bytes 3145736 | tf_op jit(solution)/shard_map/ppermute | solution.py:78
  167.8 23.3 %collective-permute-start.12 = (bf16[128,4096]{1,0:T(8,128)(2,1)S(1)}, bf16[128,4096]{1,0:T(8,128)(2,1)S(1)}, u32[]{:S(2)}, u32[]{:S(2)}) collective-permute-start(bf16[128,4096]{1,0:T(8,128)(2,1)S(1)} %collective-permute-done.10), channel_id=1, source_target_pairs={{0,16},{16,32},{32,48},{48,64},{64,80},{80,96},{96,112},{112,128},... | collective-permute-start | bytes 3145736 | tf_op jit(solution)/shard_map/ppermute | solution.py:73
  172.9 22.7 %collective-permute-start.13 = (bf16[128,4096]{1,0:T(8,128)(2,1)S(1)}, bf16[128,4096]{1,0:T(8,128)(2,1)S(1)}, u32[]{:S(2)}, u32[]{:S(2)}) collective-permute-start(bf16[128,4096]{1,0:T(8,128)(2,1)S(1)} %collective-permute-done.11), channel_id=1, source_target_pairs={{0,240},{16,0},{32,16},{48,32},{64,48},{80,64},{96,80},{112,96},{1... | collective-permute-start | bytes 3145736 | tf_op jit(solution)/shard_map/ppermute | solution.py:78
  191.2 22.1 %collective-permute-start.14 = (bf16[128,4096]{1,0:T(8,128)(2,1)S(1)}, bf16[128,4096]{1,0:T(8,128)(2,1)S(1)}, u32[]{:S(2)}, u32[]{:S(2)}) collective-permute-start(bf16[128,4096]{1,0:T(8,128)(2,1)S(1)} %collective-permute-done.12), channel_id=1, source_target_pairs={{0,16},{16,32},{32,48},{48,64},{64,80},{80,96},{96,112},{112,128},... | collective-permute-start | bytes 3145736 | tf_op jit(solution)/shard_map/ppermute | solution.py:73
Sparse Core Ops, SparseCore 0:
  9.1 62.5 all-gather.2
  73.5 62.6 all-gather.4
